TPU v7x, 32 devices: a whole 2x2x4 slice. The times are simulated.
32 devices in a mesh: section: 4 (over y, x), ctx: 4 (over z), tp: 2 (over core).
Axes of the slice: x: 2, y: 2, z: 4, core: 2. Of those that a mesh axis runs over, the one named last changes fastest.
Arguments:
- queries: bfloat16 [2048, 8, 8, 128], P('ctx', 'tp', 'section'), may hold values from -44 to 44
- key_states: bfloat16 [2048, 8, 128], P('ctx', 'tp'), may hold values from -4 to 4
- value_states: bfloat16 [2048, 8, 128], P('ctx', 'tp'), may hold values from -6 to 6
- out_grad: bfloat16 [2048, 8, 8, 128], P('ctx', 'tp', 'section'), may hold values from -6 to 6
- band_offsets: int32 [16, 3], replicated, may hold values from -1 to 4, as said below
- global_blocks: int32 [16, 4], replicated, may hold values from -1 to 8, as said below
Outputs:
- attended: bfloat16 [2048, 8, 8, 128], P('ctx', 'tp', 'section')
- query_grad: float32 [2048, 8, 8, 128], P('ctx', 'tp', 'section')
- key_grad: float32 [2048, 8, 128], P('ctx', 'tp')
- value_grad: float32 [2048, 8, 128], P('ctx', 'tp')
Inputs may be any that keep to these rules, and one draw needn't show every extreme that they name: `band_offsets`: in every row r the first offset is 0, the second lies in 1 to 2 and the third in 3 to 4; an offset larger than r is replaced by -1. `global_blocks`: entry n of row r is either -1 or n * 4, and it is n * 4 only when n * 4 < r - 4.
All inputs are finite; a program needn't handle non-finite values.
Results may differ from a plain program's by a relative error of at most 0.017.
Values may be sent and summed in bfloat16 or wider, within the bound.
A program may use at most 128 MiB of HBM per device.

v0:
```python
import jax
import jax.numpy as jnp
from jax import lax
from jax.sharding import PartitionSpec as P

BLK = 128
NBAND = 3
NGLOB = 4


def passed_along(shard, axis, by):
    count = lax.axis_size(axis)
    pairs = [(i, i + by) for i in range(count) if 0 <= i + by < count]
    return lax.ppermute(shard, axis, pairs)


def shards(queries, key_states, value_states, out_grad, band_offsets, global_blocks):
    tok_rows, kv_local, group_local, head_dim = queries.shape
    own_blocks = tok_rows // BLK
    ctx_count = lax.axis_size("ctx")
    all_blocks = own_blocks * ctx_count
    stride_blocks = all_blocks // NGLOB
    stride_devices = stride_blocks // own_blocks
    position = lax.axis_index("ctx")
    scale_factor = head_dim ** (-0.5)
    paired = jnp.stack([key_states, value_states])
    earlier = passed_along(paired, "ctx", 1)
    leading = paired[:, :BLK]
    every_first = lax.all_gather(leading, "ctx", axis=1, tiled=True)
    grouped = every_first.reshape(2, ctx_count, BLK, kv_local, head_dim)[:, ::stride_devices]
    global_rows = grouped.reshape(2, NGLOB * BLK, kv_local, head_dim)
    buffer_blocks = 2 * own_blocks + NGLOB
    stacked = jnp.concatenate([earlier, paired, global_rows], axis=1).reshape(
        2, buffer_blocks, BLK, kv_local, head_dim
    )
    offsets = lax.dynamic_slice_in_dim(band_offsets, position * own_blocks, own_blocks, 0)
    chosen_globals = lax.dynamic_slice_in_dim(global_blocks, position * own_blocks, own_blocks, 0)
    local_rows = jnp.arange(own_blocks, dtype=jnp.int32)[:, None]
    band_ids = own_blocks + local_rows - offsets
    glob_ids = 2 * own_blocks + chosen_globals // stride_blocks
    usable = jnp.concatenate([offsets >= 0, chosen_globals >= 0], axis=1)
    block_ids = jnp.where(usable, jnp.concatenate([band_ids, glob_ids], axis=1), 0)
    key_sel = stacked[0][block_ids]
    value_sel = stacked[1][block_ids]
    query_rows = queries.reshape(own_blocks, BLK, kv_local, group_local, head_dim)
    grad_rows = out_grad.reshape(own_blocks, BLK, kv_local, group_local, head_dim)
    scores = (
        jnp.einsum("rihgd,rnjhd->rhginj", query_rows, key_sel, preferred_element_type=jnp.float32)
        * scale_factor
    )
    lower_half = jnp.arange(BLK)[:, None] >= jnp.arange(BLK)[None, :]
    first_slot = jnp.arange(NBAND + NGLOB) == 0
    reach = jnp.logical_not(first_slot)[None, :, None] | lower_half[:, None, :]
    allowed = usable[:, None, None, None, :, None] & reach[None, None, None]
    scores = jnp.where(allowed, scores, -jnp.inf)
    row_top = jnp.max(scores, axis=(4, 5), keepdims=True)
    probs = jnp.exp(scores - row_top)
    row_total = jnp.sum(probs, axis=(4, 5), keepdims=True)
    weights = probs / row_total
    weights_low = weights.astype(jnp.bfloat16)
    attended = jnp.einsum(
        "rhginj,rnjhd->rihgd", weights_low, value_sel, preferred_element_type=jnp.float32
    ).astype(jnp.bfloat16)
    row_dots = jnp.sum(grad_rows.astype(jnp.float32) * attended.astype(jnp.float32), axis=-1)
    row_dots = jnp.transpose(row_dots, (0, 2, 3, 1))
    dweights = jnp.einsum(
        "rihgd,rnjhd->rhginj", grad_rows, value_sel, preferred_element_type=jnp.float32
    )
    dscores = (weights * (dweights - row_dots[..., None, None])).astype(jnp.bfloat16)
    query_grad = scale_factor * jnp.einsum(
        "rhginj,rnjhd->rihgd", dscores, key_sel, preferred_element_type=jnp.float32
    )
    key_part = scale_factor * jnp.einsum(
        "rhginj,rihgd->rnjhd", dscores, query_rows, preferred_element_type=jnp.float32
    )
    value_part = jnp.einsum(
        "rhginj,rihgd->rnjhd", weights_low, grad_rows, preferred_element_type=jnp.float32
    )
    slot_count = own_blocks * (NBAND + NGLOB)
    target_ids = jnp.where(usable, block_ids, buffer_blocks).reshape(slot_count)

    def place_blocks(part_grad):
        flat_grad = part_grad.reshape(slot_count, BLK, kv_local, head_dim)
        placed = jax.ops.segment_sum(flat_grad, target_ids, num_segments=buffer_blocks + 1)
        return placed[:buffer_blocks]

    block_grads = jnp.stack([place_blocks(key_part), place_blocks(value_part)])
    earlier_grads = block_grads[:, :own_blocks].reshape(2, tok_rows, kv_local, head_dim)
    own_grads = block_grads[:, own_blocks : 2 * own_blocks].reshape(2, tok_rows, kv_local, head_dim)
    global_grads = block_grads[:, 2 * own_blocks :]
    returned = passed_along(earlier_grads.astype(jnp.bfloat16), "ctx", -1).astype(
        earlier_grads.dtype
    )
    own_grads = own_grads + returned
    owner_mask = (jnp.arange(NGLOB) * stride_devices == position).astype(jnp.float32)
    summed = lax.psum(global_grads.astype(jnp.bfloat16), "ctx").astype(jnp.float32)
    owner_rows = jnp.einsum("g,cgjhd->cjhd", owner_mask, summed, precision=lax.Precision.HIGHEST)
    totals = lax.psum(
        jnp.concatenate([own_grads[:, :BLK] + owner_rows, own_grads[:, BLK:]], axis=1), "section"
    )
    return (
        attended.reshape(tok_rows, kv_local, group_local, head_dim),
        query_grad.reshape(tok_rows, kv_local, group_local, head_dim),
        totals[0],
        totals[1],
    )


def solution(mesh):
    placed = (
        P("ctx", "tp", "section", None),
        P("ctx", "tp", None),
        P("ctx", "tp", None),
        P("ctx", "tp", "section", None),
        P(),
        P(),
    )
    return jax.shard_map(
        shards,
        mesh=mesh,
        in_specs=placed,
        out_specs=(
            P("ctx", "tp", "section", None),
            P("ctx", "tp", "section", None),
            P("ctx", "tp", None),
            P("ctx", "tp", None),
        ),
        check_vma=False,
    )
```

profile of v0, /device:TPU:0, one launch (start us, length us, event | category | flops | bytes accessed | tf_op | source)
XLA Modules:
  0.0 332.9 jit_solution(10869660269288517391)
XLA Ops:
  7.3 1.5 copy_bitcast_fusion
  8.7 0.7 fusion.38
  9.5 1.1 pad_maximum_fusion.3
  10.6 6.0 %collective-permute-start = (bf16[2,512,4,128]{3,1,2,0:T(8,128)(2,1)}, bf16[2,512,4,128]{3,1,2,0:T(8,128)(2,1)}, u32[]{:S(2)}, u32[]{:S(2)}) collective-permute-start(bf16[2,512,4,128]{3,1,2,0:T(8,128)(2,1)} %pad_maximum_fusion.3), channel_id=1, source_target_pairs={{0,2},{2,4},{4,6},{1,3},{3,5},{5,7},{8,10},{10,12},{12,14},{9,11},... | collective-permute-start | bytes 3145736 | tf_op jit(solution)/shard_map/ppermute | solution.py:14
  16.6 0.1 fusion.40
  16.7 0.1 copy.84
  16.8 0.1 copy.83
  17.0 0.1 copy.82
  17.2 0.1 copy.81
  17.3 0.1 compare_select_fusion
  17.4 1.1 copy.93
  18.5 0.1 copy.86
  18.6 0.1 reshape.167
  18.7 0.1 concatenate.50
  18.8 0.1 copy.101
  18.9 0.1 concatenate.52
  19.0 0.1 broadcast_or_fusion
  19.2 0.3 broadcast_and_fusion
  19.4 35.7 %collective-permute-done = bf16[2,512,4,128]{3,1,2,0:T(8,128)(2,1)} collective-permute-done((bf16[2,512,4,128]{3,1,2,0:T(8,128)(2,1)}, bf16[2,512,4,128]{3,1,2,0:T(8,128)(2,1)}, u32[]{:S(2)}, u32[]{:S(2)}) %collective-permute-start) | collective-permute-done | bytes 1048608 | tf_op jit(solution)/shard_map/ppermute | solution.py:14
  55.1 1.6 pad_maximum_fusion.1
  56.8 1.3 fusion.46
  58.1 0.1 copy.87
  58.2 2.9 gather_fusion.1
  61.1 8.5 %fusion.4 = (f32[4,4,2,128]{3,2,1,0:T(2,128)S(1)}, f32[4,4,7,128,128,2]{4,3,5,2,1,0:T(8,128)}) fusion(pred[4,128,7,128]{1,3,2,0:T(8,128)(4,1)S(1)} %broadcast_and_fusion, bf16[4,128,4,2,128,1]{4,3,2,1,0,5:T(2,128)(2,1)S(1)} %bitcast.99, bf16[4,7,128,4,128,1]{4,2,3,1,0,5:T(8,128)(2,1)} %bitcast.110), kind=kOutput, calls=%fused_computation.11 | convolution fusion | flops 950530048 | bytes 19873792 | tf_op jit(solution)/shard_map/rihgd,rnjhd->rhginj/dot_general | solution.py:48
  69.5 8.2 %fusion.3 = f32[4,4,2,128]{3,2,1,0:T(2,128)S(1)} fusion(f32[4,4,7,128,128,2]{4,3,5,2,1,0:T(8,128)} %get-tuple-element.23, f32[4,4,2,128]{3,2,1,0:T(2,128)S(1)} %get-tuple-element.22, pred[4,128,7,128]{1,3,2,0:T(8,128)(4,1)S(1)} %broadcast_and_fusion), kind=kLoop, calls=%fused_computation.10 | loop fusion | flops 14675968 | bytes 15171584 | tf_op jit(solution)/shard_map/reduce_sum | solution.py:58
  77.8 9.6 %fusion.16 = bf16[4,4,2,128,7,128]{3,5,2,4,1,0:T(8,128)(2,1)} fusion(f32[4,4,2,128]{3,2,1,0:T(2,128)S(1)} %fusion.3, f32[4,4,2,128]{3,2,1,0:T(2,128)S(1)} %get-tuple-element.22, f32[4,4,7,128,128,2]{4,3,5,2,1,0:T(8,128)} %get-tuple-element.23, pred[4,128,7,128]{1,3,2,0:T(8,128)(4,1)S(1)} %broadcast_and_fusion), kind=kLoop, calls=%fused_computation.31 | loop fusion | flops 18350080 | bytes 22511616 | tf_op jit(solution)/shard_map/convert_element_type | solution.py:60
  87.4 0.1 copy.85
  87.5 2.9 gather_fusion
  90.4 8.5 %convolution_bitcast_fusion = f32[4,7,128,4,128]{4,2,1,3,0:T(8,128)} fusion(bf16[4,4,2,128,7,128]{3,5,2,4,1,0:T(8,128)(2,1)} %fusion.16, bf16[4,128,4,2,128,1]{4,1,0,3,2,5:T(8,128)(2,1)} %bitcast.107), kind=kOutput, calls=%fused_computation.30 | convolution fusion | flops 939524096 | bytes 15728640 | tf_op jit(solution)/shard_map/rhginj,rihgd->rnjhd/dot_general | solution.py:76
  98.8 6.6 %multiply_reduce_fusion = (f32[4,128,4,2]{1,3,2,0:T(2,128)S(1)}, bf16[4,128,4,2,128]{4,1,3,2,0:T(8,128)(2,1)}) fusion(bf16[4,128,4,2,128]{4,1,0,3,2:T(8,128)(2,1)S(1)} %bitcast.108, bf16[4,4,2,128,7,128]{3,5,2,4,1,0:T(8,128)(2,1)} %fusion.16, bf16[4,7,128,4,128,1]{4,2,3,1,0,5:T(8,128)(2,1)S(1)} %bitcast.112), kind=kOutput, calls=%fused_computation.38 | convolution fusion | flops 942141440 | bytes 13123584 | tf_op jit(solution)/shard_map/rhginj,rnjhd->rihgd/dot_general | solution.py:61
  105.5 8.0 %fusion.1 = bf16[4,4,2,128,7,128]{3,5,2,4,1,0:T(8,128)(2,1)S(1)} fusion(f32[4,4,2,128]{3,2,1,0:T(2,128)S(1)} %bitcast.119, bf16[4,7,128,4,128,1]{4,2,3,1,0,5:T(8,128)(2,1)S(1)} %bitcast.113, f32[4,4,2,128]{3,2,1,0:T(2,128)S(1)} %fusion.3, f32[4,4,2,128]{3,2,1,0:T(2,128)S(1)} %get-tuple-element.22, f32[4,4,7,128,128,2]{4,3,5,2,1,0:T(8,128)} %get-tuple-element.23, ...), kind=kOutput, calls=%fused_computation.6 | convolution fusion | flops 965214208 | bytes 27246592 | tf_op jit(solution)/shard_map/rihgd,rnjhd->rhginj/dot_general | solution.py:66
  113.5 2.1 fusion.5
  115.6 0.8 copy-done.4
  116.4 4.0 %copy.103 = f32[4,7,128,4,128]{4,2,3,1,0:T(8,128)} copy(f32[4,7,128,4,128]{4,2,1,3,0:T(8,128)S(1)} %fusion.5) | data formatting | bytes 14680064 | tf_op jit(solution)/shard_map/mul | solution.py:73
  120.4 2.2 broadcast.117.clone
  122.6 17.9 %scatter_fusion = f32[13,128,4,128]{3,1,2,0:T(8,128)} fusion(f32[13,128,4,128]{3,1,2,0:T(8,128)} %broadcast.117.clone, s32[28]{0:T(128)S(1)} %fusion.42, f32[28,128,4,128]{3,1,2,0:T(8,128)} %bitcast.102), kind=kCustom, calls=%fused_computation.2 | custom fusion | flops 1835008 | bytes 22020208 | tf_op jit(solution)/shard_map/scatter-add | solution.py:84
  140.5 3.9 %slice_bitcast_fusion.1 = f32[1,12,128,4,128]{4,2,3,1,0:T(8,128)} fusion(f32[13,128,4,128]{3,1,2,0:T(8,128)} %scatter_fusion), kind=kLoop, calls=%fused_computation.28 | loop fusion | bytes 6291456 | tf_op jit(solution)/shard_map/stack | solution.py:87
  144.4 7.0 %copy.105 = f32[4,7,128,4,128]{4,2,3,1,0:T(8,128)} copy(f32[4,7,128,4,128]{4,2,1,3,0:T(8,128)} %convolution_bitcast_fusion) | data formatting | bytes 14680064 | tf_op jit(solution)/shard_map/rhginj,rihgd->rnjhd/transpose | solution.py:76
  151.5 2.1 broadcast.117.clone.1
  153.6 17.2 %scatter_fusion.1 = f32[13,128,4,128]{3,1,2,0:T(8,128)} fusion(f32[13,128,4,128]{3,1,2,0:T(8,128)} %broadcast.117.clone.1, s32[28]{0:T(128)S(1)} %fusion.42, f32[28,128,4,128]{3,1,2,0:T(8,128)} %bitcast.101), kind=kCustom, calls=%fused_computation.3 | custom fusion | flops 1835008 | bytes 22020208 | tf_op jit(solution)/shard_map/scatter-add | solution.py:84
  170.8 2.2 slice_bitcast_fusion
  173.0 0.6 copy-done.2
  173.6 0.6 fusion.10
  174.2 1.1 copy-done.3
  175.3 1.1 fusion.45
  176.5 1.3 collective-permute-start.1
  177.8 0.3 all-reduce.5.cloned.1.call-start
  178.1 1.7 fusion.17
  179.8 0.2 copy.106
  180.0 40.9 %collective-permute-done.1 = bf16[2,512,4,128]{3,1,2,0:T(8,128)(2,1)S(1)} collective-permute-done((bf16[2,512,4,128]{3,1,2,0:T(8,128)(2,1)S(1)}, bf16[2,512,4,128]{3,1,2,0:T(8,128)(2,1)S(1)}, u32[]{:S(2)}, u32[]{:S(2)}) %collective-permute-start.1) | collective-permute-done | bytes 1048608 | tf_op jit(solution)/shard_map/ppermute | solution.py:14
  220.9 0.2 bitcast_add_fusion
  221.1 1.3 slice.67
  222.4 26.3 %all-reduce.3.cloned.1.call-done = bf16[2,4,128,4,128]{4,2,3,1,0:T(8,128)(2,1)} async-done(((bf16[2,4,128,4,128]{4,2,3,1,0:T(8,128)(2,1)}), bf16[2,4,128,4,128]{4,2,3,1,0:T(8,128)(2,1)}) %all-reduce.3.cloned.1.call-update) | async-done | bytes 1048592 | tf_op jit(solution)/shard_map/psum | solution.py:96
  248.7 2.2 fusion.32
  251.0 1.5 pad_maximum_fusion.2
  252.5 0.1 copy-done.11
  252.7 2.0 copy.108
  254.7 5.9 %fusion.18 = f32[4,128,4,2,128]{4,1,3,2,0:T(8,128)S(1)} fusion(bf16[4,4,2,128,7,128]{3,5,2,4,1,0:T(8,128)(2,1)} %copy-done.4, bf16[4,7,128,4,128,1]{4,2,3,1,0,5:T(8,128)(2,1)S(1)} %bitcast.111), kind=kOutput, calls=%fused_computation.36 | convolution fusion | flops 940048384 | bytes 13107200 | tf_op jit(solution)/shard_map/rhginj,rnjhd->rihgd/dot_general | solution.py:70
  260.6 0.2 copy.99
  260.9 2.9 copy.109
  263.8 57.6 %all-reduce.5.cloned.1.call-done = f32[2,512,4,128]{3,1,2,0:T(8,128)} async-done(((f32[2,512,4,128]{3,1,2,0:T(8,128)}), f32[2,512,4,128]{3,1,2,0:T(8,128)}) %all-reduce.5.cloned.1.call-update) | async-done | bytes 2097168 | tf_op jit(solution)/shard_map/psum | solution.py:98
  321.4 1.7 slice_bitcast_fusion.2
  323.1 1.6 copy.110
  324.8 1.6 copy.111
  (43 shorter events, 0.7 us)
Async XLA Ops:
  7.2 53.9 %copy-start = (bf16[512,4,2,128]{3,2,1,0:T(2,128)(2,1)S(1)}, bf16[512,4,2,128]{3,2,1,0:T(2,128)(2,1)}, u32[]{:S(2)}) copy-start(bf16[512,4,2,128]{3,2,1,0:T(2,128)(2,1)} %param.6) | copy-start | bytes 3145732
  7.2 9.4 %copy-start.12 = (s32[16,4]{0,1:T(4,128)S(1)}, s32[16,4]{0,1:T(4,128)}, u32[]{:S(2)}) copy-start(s32[16,4]{0,1:T(4,128)} %param.11) | copy-start | bytes 772
  7.2 9.6 %copy-start.13 = (s32[16,3]{0,1:T(4,128)S(1)}, s32[16,3]{0,1:T(4,128)}, u32[]{:S(2)}) copy-start(s32[16,3]{0,1:T(4,128)} %param.10) | copy-start | bytes 580
  7.2 10.2 %copy-start.10 = (bf16[512,4,2,128]{3,2,1,0:T(2,128)(2,1)S(1)}, bf16[512,4,2,128]{3,2,1,0:T(2,128)(2,1)}, u32[]{:S(2)}) copy-start(bf16[512,4,2,128]{3,2,1,0:T(2,128)(2,1)} %param.9) | copy-start | bytes 3145732
  7.2 47.9 %all-gather.2.cloned.1.call-start = ((), (), s32[]{:S(2)}) async-start(), calls=%async_computation | async-start | bytes 1310720 | tf_op jit(solution)/shard_map/all_gather | solution.py:29
  9.5 239.2 %all-reduce.3.cloned.1.call-start = ((), (), s32[]{:S(2)}) async-start(), calls=%async_computation.1 | async-start | bytes 2097152 | tf_op jit(solution)/shard_map/psum | solution.py:96
  10.6 44.5 %collective-permute-start = (bf16[2,512,4,128]{3,1,2,0:T(8,128)(2,1)}, bf16[2,512,4,128]{3,1,2,0:T(8,128)(2,1)}, u32[]{:S(2)}, u32[]{:S(2)}) collective-permute-start(bf16[2,512,4,128]{3,1,2,0:T(8,128)(2,1)} %pad_maximum_fusion.3), channel_id=1, source_target_pairs={{0,2},{2,4},{4,6},{1,3},{3,5},{5,7},{8,10},{10,12},{12,14},{9,11},... | collective-permute-start | bytes 3145736 | tf_op jit(solution)/shard_map/ppermute | solution.py:14
  77.8 9.6 %copy-start.5 = (bf16[1,1536,4,128]{3,1,2,0:T(8,128)(2,1)S(1)}, bf16[1,1536,4,128]{3,1,2,0:T(8,128)(2,1)}, u32[]{:S(2)}) copy-start(bf16[1,1536,4,128]{3,1,2,0:T(8,128)(2,1)} %get-tuple-element.18) | copy-start | bytes 4718596
  90.4 8.5 %copy-start.7 = (bf16[512,4,2,128]{3,0,2,1:T(8,128)(2,1)S(1)}, bf16[512,4,2,128]{3,0,2,1:T(8,128)(2,1)}, u32[]{:S(2)}) copy-start(bf16[512,4,2,128]{3,0,2,1:T(8,128)(2,1)} %copy.93) | copy-start | bytes 3145732
  90.4 8.5 %copy-start.9 = (bf16[28,128,4,128]{3,1,2,0:T(8,128)(2,1)S(1)}, bf16[28,128,4,128]{3,1,2,0:T(8,128)(2,1)}, u32[]{:S(2)}) copy-start(bf16[28,128,4,128]{3,1,2,0:T(8,128)(2,1)} %gather_fusion) | copy-start | bytes 11010052
  113.5 2.9 copy-start.4
  170.8 2.8 copy-start.2
  173.6 1.7 copy-start.3
  176.5 44.4 %collective-permute-start.1 = (bf16[2,512,4,128]{3,1,2,0:T(8,128)(2,1)S(1)}, bf16[2,512,4,128]{3,1,2,0:T(8,128)(2,1)S(1)}, u32[]{:S(2)}, u32[]{:S(2)}) collective-permute-start(bf16[2,512,4,128]{3,1,2,0:T(8,128)(2,1)S(1)} %bitcast.114), channel_id=1, source_target_pairs={{2,0},{4,2},{6,4},{3,1},{5,3},{7,5},{10,8},{12,10},{14,12},{11,9},... | collective-permute-start | bytes 3145736 | tf_op jit(solution)/shard_map/ppermute | solution.py:14
  177.8 143.6 %all-reduce.5.cloned.1.call-start = ((), (), s32[]{:S(2)}) async-start(), calls=%async_computation.2 | async-start | bytes 4194304 | tf_op jit(solution)/shard_map/psum | solution.py:98
  248.7 2.3 copy-start.6
  251.0 1.6 copy-start.11
  252.5 2.2 copy-start.8
  260.8 65.6 %copy-start.1 = (bf16[512,4,2,128]{3,2,1,0:T(2,128)(2,1)S(1)}, bf16[512,4,2,128]{3,2,1,0:T(2,128)(2,1)}, u32[]{:S(2)}) copy-start(bf16[512,4,2,128]{3,2,1,0:T(2,128)(2,1)} %param.6) | copy-start | bytes 3145732
Sparse Core Ops, SparseCore 0:
  10.2 44.1 all-gather.1
  177.9 70.7 all-reduce.2
  252.6 68.7 all-reduce.4
where the time goes:
time: 334 us; the launch traced here: 333 us
  waiting for transfers between devices  161 us (48%)
  other arithmetic  61.2 us (18%)
  local copies, waits for them, and re-layouts  47.8 us (14%)
  matrix products  41.8 us (13%)
  between operations  14 us (4%)
  starting transfers between devices  7.61 us (2%)
    ppermute x2, waiting for transfers between devices, passed_along(): return lax.ppermute(shard, axis, pairs)  76.6 us
    psum x1, waiting for transfers between devices, shards(): lax.psum(jnp.concatenate([own_grads[:, :BLK] + owner_rows, own_grads[:, B...  57.6 us
    scatter-add x2, other arithmetic, place_blocks(): jax.ops.segment_sum(flat_grad, target_ids, num_segments=buffer_blocks + 1)  35 us
    psum x1, waiting for transfers between devices, shards(): lax.psum(global_grads.astype(jnp.bfloat16), 'ctx').astype(jnp.float32)  26.3 us
    unnamed x33, local copies, waits for them, and re-layouts  12 us
    convert_element_type x1, other arithmetic, shards(): weights_low = weights.astype(jnp.bfloat16)  9.61 us
    dot_general x1, matrix products, shards(): jnp.einsum('rihgd,rnjhd->rhginj', query_rows, key_sel, preferred_element_...  8.46 us
    dot_general x1, matrix products, shards(): jnp.einsum('rhginj,rihgd->rnjhd', weights_low, grad_rows, preferred_eleme...  8.45 us
  transfers between devices with their start and end apart: 5, of which 4 were waited for; matrix products, arithmetic and copies ran while one was open for 6% of the time, Pallas kernels for 0%

commit v1 on v0

--- a/solution.py
+++ b/solution.py
@@ -95,8 +95,12 @@
     owner_mask = (jnp.arange(NGLOB) * stride_devices == position).astype(jnp.float32)
     summed = lax.psum(global_grads.astype(jnp.bfloat16), "ctx").astype(jnp.float32)
     owner_rows = jnp.einsum("g,cgjhd->cjhd", owner_mask, summed, precision=lax.Precision.HIGHEST)
-    totals = lax.psum(
-        jnp.concatenate([own_grads[:, :BLK] + owner_rows, own_grads[:, BLK:]], axis=1), "section"
+    totals = jnp.sum(
+        lax.all_gather(
+            jnp.concatenate([own_grads[:, :BLK] + owner_rows, own_grads[:, BLK:]], axis=1),
+            "section",
+        ),
+        axis=0,
     )
     return (
         attended.reshape(tok_rows, kv_local, group_local, head_dim),

time: 334 us -> 354 us (1.060)
  waiting for transfers between devices: 161 us -> 179 us
  other arithmetic: 61.2 us -> 65.2 us
    all_gather x0 -> x1, waiting for transfers between devices: none -> 76.1 us  [shards(): lax.all_gather(jnp.concatenate([own_grads[:, :BLK] + owner_rows, own_grad...]
    psum x1 -> x0, waiting for transfers between devices: 57.6 us -> none  [shards(): lax.psum(jnp.concatenate([own_grads[:, :BLK] + owner_rows, own_grads[:, B...]
    reduce_sum x0 -> x1, other arithmetic: none -> 4.16 us  [shards(): jnp.sum(lax.all_gather(jnp.concatenate([own_grads[:, :BLK] + owner_rows,...]
  transfers between devices with their start and end apart: 5 -> 5, of which waited for: 4 -> 4; matrix products, arithmetic and copies ran while one was open for 6% -> 5% of each run, Pallas kernels for 0% -> 0%
where the time goes in v1:
time: 354 us
  waiting for transfers between devices  179 us (51%)
  other arithmetic  65.2 us (18%)
  local copies, waits for them, and re-layouts  46.2 us (13%)
  matrix products  41.4 us (12%)
  between operations  14 us (4%)
  starting transfers between devices  7.61 us (2%)
    ppermute x2, waiting for transfers between devices, passed_along(): return lax.ppermute(shard, axis, pairs)  77 us
    all_gather x1, waiting for transfers between devices, shards(): lax.all_gather(jnp.concatenate([own_grads[:, :BLK] + owner_rows, own_grad...  76.1 us
    scatter-add x2, other arithmetic, place_blocks(): jax.ops.segment_sum(flat_grad, target_ids, num_segments=buffer_blocks + 1)  34.8 us
    psum x1, waiting for transfers between devices, shards(): lax.psum(global_grads.astype(jnp.bfloat16), 'ctx').astype(jnp.float32)  26.3 us
    unnamed x33, local copies, waits for them, and re-layouts  12.1 us
    convert_element_type x1, other arithmetic, shards(): weights_low = weights.astype(jnp.bfloat16)  9.59 us
    dot_general x1, matrix products, shards(): jnp.einsum('rhginj,rihgd->rnjhd', weights_low, grad_rows, preferred_eleme...  8.53 us
    dot_general x1, matrix products, shards(): jnp.einsum('rihgd,rnjhd->rhginj', query_rows, key_sel, preferred_element_...  8.51 us
  transfers between devices with their start and end apart: 5, of which 4 were waited for; matrix products, arithmetic and copies ran while one was open for 5% of the time, Pallas kernels for 0%

profile of v1, /device:TPU:0, one launch (start us, length us, event | category | flops | bytes accessed | tf_op | source)
XLA Modules:
  0.0 353.9 jit_solution(17239822524331131653)
XLA Ops:
  7.3 1.5 copy_bitcast_fusion
  8.7 0.7 fusion.38
  9.5 1.1 pad_maximum_fusion.3
  10.6 6.0 %collective-permute-start = (bf16[2,512,4,128]{3,1,2,0:T(8,128)(2,1)}, bf16[2,512,4,128]{3,1,2,0:T(8,128)(2,1)}, u32[]{:S(2)}, u32[]{:S(2)}) collective-permute-start(bf16[2,512,4,128]{3,1,2,0:T(8,128)(2,1)} %pad_maximum_fusion.3), channel_id=1, source_target_pairs={{0,2},{2,4},{4,6},{1,3},{3,5},{5,7},{8,10},{10,12},{12,14},{9,11},... | collective-permute-start | bytes 3145736 | tf_op jit(solution)/shard_map/ppermute | solution.py:14
  16.6 0.1 fusion.40
  16.7 0.1 copy.111
  16.8 0.1 copy.110
  17.0 0.1 copy.109
  17.2 0.1 copy.108
  17.3 0.1 compare_select_fusion
  17.4 1.1 copy.120
  18.5 0.1 copy.113
  18.6 0.1 reshape.167
  18.7 0.1 concatenate.50
  18.8 0.1 copy.128
  18.9 0.1 concatenate.52
  19.0 0.1 broadcast_or_fusion
  19.2 0.3 broadcast_and_fusion
  19.4 35.7 %collective-permute-done = bf16[2,512,4,128]{3,1,2,0:T(8,128)(2,1)} collective-permute-done((bf16[2,512,4,128]{3,1,2,0:T(8,128)(2,1)}, bf16[2,512,4,128]{3,1,2,0:T(8,128)(2,1)}, u32[]{:S(2)}, u32[]{:S(2)}) %collective-permute-start) | collective-permute-done | bytes 1048608 | tf_op jit(solution)/shard_map/ppermute | solution.py:14
  55.1 1.6 pad_maximum_fusion.1
  56.8 1.3 fusion.46
  58.1 0.1 copy.114
  58.2 2.9 gather_fusion.1
  61.1 8.5 %fusion.4 = (f32[4,4,2,128]{3,2,1,0:T(2,128)S(1)}, f32[4,4,7,128,128,2]{4,3,5,2,1,0:T(8,128)}) fusion(pred[4,128,7,128]{1,3,2,0:T(8,128)(4,1)S(1)} %broadcast_and_fusion, bf16[4,128,4,2,128,1]{4,3,2,1,0,5:T(2,128)(2,1)S(1)} %bitcast.100, bf16[4,7,128,4,128,1]{4,2,3,1,0,5:T(8,128)(2,1)} %bitcast.112), kind=kOutput, calls=%fused_computation.11 | convolution fusion | flops 950530048 | bytes 19873792 | tf_op jit(solution)/shard_map/rihgd,rnjhd->rhginj/dot_general | solution.py:48
  69.6 8.2 %fusion.3 = f32[4,4,2,128]{3,2,1,0:T(2,128)S(1)} fusion(f32[4,4,7,128,128,2]{4,3,5,2,1,0:T(8,128)} %get-tuple-element.27, f32[4,4,2,128]{3,2,1,0:T(2,128)S(1)} %get-tuple-element.26, pred[4,128,7,128]{1,3,2,0:T(8,128)(4,1)S(1)} %broadcast_and_fusion), kind=kLoop, calls=%fused_computation.10 | loop fusion | flops 14675968 | bytes 15171584 | tf_op jit(solution)/shard_map/reduce_sum | solution.py:58
  77.9 9.6 %fusion.16 = bf16[4,4,2,128,7,128]{3,5,2,4,1,0:T(8,128)(2,1)} fusion(f32[4,4,2,128]{3,2,1,0:T(2,128)S(1)} %fusion.3, f32[4,4,2,128]{3,2,1,0:T(2,128)S(1)} %get-tuple-element.26, f32[4,4,7,128,128,2]{4,3,5,2,1,0:T(8,128)} %get-tuple-element.27, pred[4,128,7,128]{1,3,2,0:T(8,128)(4,1)S(1)} %broadcast_and_fusion), kind=kLoop, calls=%fused_computation.31 | loop fusion | flops 18350080 | bytes 22511616 | tf_op jit(solution)/shard_map/convert_element_type | solution.py:60
  87.5 0.1 copy.112
  87.6 2.9 gather_fusion
  90.4 8.5 %convolution_bitcast_fusion = f32[4,7,128,4,128]{4,2,1,3,0:T(8,128)} fusion(bf16[4,4,2,128,7,128]{3,5,2,4,1,0:T(8,128)(2,1)} %fusion.16, bf16[4,128,4,2,128,1]{4,1,0,3,2,5:T(8,128)(2,1)} %bitcast.109), kind=kOutput, calls=%fused_computation.30 | convolution fusion | flops 939524096 | bytes 15728640 | tf_op jit(solution)/shard_map/rhginj,rihgd->rnjhd/dot_general | solution.py:76
  99.0 6.6 %multiply_reduce_fusion = (f32[4,128,4,2]{1,3,2,0:T(2,128)S(1)}, bf16[4,128,4,2,128]{4,1,3,2,0:T(8,128)(2,1)}) fusion(bf16[4,128,4,2,128]{4,1,0,3,2:T(8,128)(2,1)S(1)} %bitcast.110, bf16[4,4,2,128,7,128]{3,5,2,4,1,0:T(8,128)(2,1)} %fusion.16, bf16[4,7,128,4,128,1]{4,2,3,1,0,5:T(8,128)(2,1)S(1)} %bitcast.114), kind=kOutput, calls=%fused_computation.38 | convolution fusion | flops 942141440 | bytes 13123584 | tf_op jit(solution)/shard_map/rhginj,rnjhd->rihgd/dot_general | solution.py:61
  105.6 8.0 %fusion.1 = bf16[4,4,2,128,7,128]{3,5,2,4,1,0:T(8,128)(2,1)S(1)} fusion(f32[4,4,2,128]{3,2,1,0:T(2,128)S(1)} %bitcast.121, bf16[4,7,128,4,128,1]{4,2,3,1,0,5:T(8,128)(2,1)S(1)} %bitcast.115, f32[4,4,2,128]{3,2,1,0:T(2,128)S(1)} %fusion.3, f32[4,4,2,128]{3,2,1,0:T(2,128)S(1)} %get-tuple-element.26, f32[4,4,7,128,128,2]{4,3,5,2,1,0:T(8,128)} %get-tuple-element.27, ...), kind=kOutput, calls=%fused_computation.6 | convolution fusion | flops 965214208 | bytes 27246592 | tf_op jit(solution)/shard_map/rihgd,rnjhd->rhginj/dot_general | solution.py:66
  113.6 2.1 fusion.5
  115.7 0.9 copy-done.4
  116.7 4.0 %copy.130 = f32[4,7,128,4,128]{4,2,3,1,0:T(8,128)} copy(f32[4,7,128,4,128]{4,2,1,3,0:T(8,128)S(1)} %fusion.5) | data formatting | bytes 14680064 | tf_op jit(solution)/shard_map/mul | solution.py:73
  120.6 2.1 broadcast.117.clone
  122.8 17.6 %scatter_fusion = f32[13,128,4,128]{3,1,2,0:T(8,128)} fusion(f32[13,128,4,128]{3,1,2,0:T(8,128)} %broadcast.117.clone, s32[28]{0:T(128)S(1)} %fusion.42, f32[28,128,4,128]{3,1,2,0:T(8,128)} %bitcast.103), kind=kCustom, calls=%fused_computation.2 | custom fusion | flops 1835008 | bytes 22020208 | tf_op jit(solution)/shard_map/scatter-add | solution.py:84
  140.4 3.9 %slice_bitcast_fusion.1 = f32[1,12,128,4,128]{4,2,3,1,0:T(8,128)} fusion(f32[13,128,4,128]{3,1,2,0:T(8,128)} %scatter_fusion), kind=kLoop, calls=%fused_computation.28 | loop fusion | bytes 6291456 | tf_op jit(solution)/shard_map/stack | solution.py:87
  144.3 7.0 %copy.132 = f32[4,7,128,4,128]{4,2,3,1,0:T(8,128)} copy(f32[4,7,128,4,128]{4,2,1,3,0:T(8,128)} %convolution_bitcast_fusion) | data formatting | bytes 14680064 | tf_op jit(solution)/shard_map/rhginj,rihgd->rnjhd/transpose | solution.py:76
  151.3 2.2 broadcast.117.clone.1
  153.5 17.2 %scatter_fusion.1 = f32[13,128,4,128]{3,1,2,0:T(8,128)} fusion(f32[13,128,4,128]{3,1,2,0:T(8,128)} %broadcast.117.clone.1, s32[28]{0:T(128)S(1)} %fusion.42, f32[28,128,4,128]{3,1,2,0:T(8,128)} %bitcast.102), kind=kCustom, calls=%fused_computation.3 | custom fusion | flops 1835008 | bytes 22020208 | tf_op jit(solution)/shard_map/scatter-add | solution.py:84
  170.7 2.2 slice_bitcast_fusion
  172.9 0.6 copy-done.2
  173.5 0.6 fusion.10
  174.1 1.1 copy-done.3
  175.3 1.1 fusion.45
  176.4 1.3 collective-permute-start.1
  177.8 0.3 all-gather.6.cloned.1.call-start
  178.0 1.7 fusion.17
  179.7 0.2 copy.133
  179.9 41.3 %collective-permute-done.1 = bf16[2,512,4,128]{3,1,2,0:T(8,128)(2,1)S(1)} collective-permute-done((bf16[2,512,4,128]{3,1,2,0:T(8,128)(2,1)S(1)}, bf16[2,512,4,128]{3,1,2,0:T(8,128)(2,1)S(1)}, u32[]{:S(2)}, u32[]{:S(2)}) %collective-permute-start.1) | collective-permute-done | bytes 1048608 | tf_op jit(solution)/shard_map/ppermute | solution.py:14
  221.2 0.2 bitcast_add_fusion
  221.5 1.3 slice.67
  222.7 26.3 %all-reduce.2.cloned.1.call-done = bf16[2,4,128,4,128]{4,2,3,1,0:T(8,128)(2,1)} async-done(((bf16[2,4,128,4,128]{4,2,3,1,0:T(8,128)(2,1)}), bf16[2,4,128,4,128]{4,2,3,1,0:T(8,128)(2,1)}) %all-reduce.2.cloned.1.call-update) | async-done | bytes 1048592 | tf_op jit(solution)/shard_map/psum | solution.py:96
  249.0 2.2 fusion.32
  251.4 1.5 pad_maximum_fusion.2
  253.0 2.0 copy.135
  255.1 5.4 %fusion.18 = f32[4,128,4,2,128]{4,1,3,2,0:T(8,128)S(1)} fusion(bf16[4,4,2,128,7,128]{3,5,2,4,1,0:T(8,128)(2,1)} %copy-done.4, bf16[4,7,128,4,128,1]{4,2,3,1,0,5:T(8,128)(2,1)S(1)} %bitcast.113), kind=kOutput, calls=%fused_computation.36 | convolution fusion | flops 940048384 | bytes 13107200 | tf_op jit(solution)/shard_map/rhginj,rnjhd->rihgd/dot_general | solution.py:70
  260.5 0.2 copy.126
  260.7 2.9 copy.136
  263.6 76.1 %all-gather.6.cloned.1.call-done = f32[8,512,4,128]{3,1,2,0:T(8,128)} async-done(((f32[2,512,4,128]{3,1,2,0:T(8,128)}), f32[8,512,4,128]{3,1,2,0:T(8,128)}) %all-gather.6.cloned.1.call-update) | async-done | bytes 8388624 | tf_op jit(solution)/shard_map/all_gather | solution.py:99
  339.8 4.2 %reduce_sum.29 = f32[2,512,4,128]{3,1,2,0:T(8,128)S(1)} reduce(f32[4,2,512,4,128]{4,2,3,1,0:T(8,128)} %bitcast.104, f32[]{:T(128)} %constant.44.clone.1), dimensions={0}, to_apply=%region_6.7 | reduce | flops 1572864 | bytes 10485764 | tf_op jit(solution)/shard_map/reduce_sum | solution.py:98
  343.9 0.1 slice_bitcast_fusion.2
  344.1 1.6 copy.137
  345.7 1.6 copy.138
  (44 shorter events, 0.7 us)
Async XLA Ops:
  7.2 53.9 %copy-start = (bf16[512,4,2,128]{3,2,1,0:T(2,128)(2,1)S(1)}, bf16[512,4,2,128]{3,2,1,0:T(2,128)(2,1)}, u32[]{:S(2)}) copy-start(bf16[512,4,2,128]{3,2,1,0:T(2,128)(2,1)} %param.6) | copy-start | bytes 3145732
  7.2 9.4 %copy-start.12 = (s32[16,4]{0,1:T(4,128)S(1)}, s32[16,4]{0,1:T(4,128)}, u32[]{:S(2)}) copy-start(s32[16,4]{0,1:T(4,128)} %param.11) | copy-start | bytes 772
  7.2 9.6 %copy-start.13 = (s32[16,3]{0,1:T(4,128)S(1)}, s32[16,3]{0,1:T(4,128)}, u32[]{:S(2)}) copy-start(s32[16,3]{0,1:T(4,128)} %param.10) | copy-start | bytes 580
  7.2 10.2 %copy-start.10 = (bf16[512,4,2,128]{3,2,1,0:T(2,128)(2,1)S(1)}, bf16[512,4,2,128]{3,2,1,0:T(2,128)(2,1)}, u32[]{:S(2)}) copy-start(bf16[512,4,2,128]{3,2,1,0:T(2,128)(2,1)} %param.9) | copy-start | bytes 3145732
  7.2 47.9 %all-gather.4.cloned.1.call-start = ((), (), s32[]{:S(2)}) async-start(), calls=%async_computation | async-start | bytes 1310720 | tf_op jit(solution)/shard_map/all_gather | solution.py:29
  9.5 239.5 %all-reduce.2.cloned.1.call-start = ((), (), s32[]{:S(2)}) async-start(), calls=%async_computation.1 | async-start | bytes 2097152 | tf_op jit(solution)/shard_map/psum | solution.py:96
  10.6 44.5 %collective-permute-start = (bf16[2,512,4,128]{3,1,2,0:T(8,128)(2,1)}, bf16[2,512,4,128]{3,1,2,0:T(8,128)(2,1)}, u32[]{:S(2)}, u32[]{:S(2)}) collective-permute-start(bf16[2,512,4,128]{3,1,2,0:T(8,128)(2,1)} %pad_maximum_fusion.3), channel_id=1, source_target_pairs={{0,2},{2,4},{4,6},{1,3},{3,5},{5,7},{8,10},{10,12},{12,14},{9,11},... | collective-permute-start | bytes 3145736 | tf_op jit(solution)/shard_map/ppermute | solution.py:14
  77.9 9.6 %copy-start.5 = (bf16[1,1536,4,128]{3,1,2,0:T(8,128)(2,1)S(1)}, bf16[1,1536,4,128]{3,1,2,0:T(8,128)(2,1)}, u32[]{:S(2)}) copy-start(bf16[1,1536,4,128]{3,1,2,0:T(8,128)(2,1)} %get-tuple-element.22) | copy-start | bytes 4718596
  90.4 8.5 %copy-start.7 = (bf16[512,4,2,128]{3,0,2,1:T(8,128)(2,1)S(1)}, bf16[512,4,2,128]{3,0,2,1:T(8,128)(2,1)}, u32[]{:S(2)}) copy-start(bf16[512,4,2,128]{3,0,2,1:T(8,128)(2,1)} %copy.120) | copy-start | bytes 3145732
  90.4 8.5 %copy-start.9 = (bf16[28,128,4,128]{3,1,2,0:T(8,128)(2,1)S(1)}, bf16[28,128,4,128]{3,1,2,0:T(8,128)(2,1)}, u32[]{:S(2)}) copy-start(bf16[28,128,4,128]{3,1,2,0:T(8,128)(2,1)} %gather_fusion) | copy-start | bytes 11010052
  113.6 3.0 copy-start.4
  170.7 2.8 copy-start.2
  173.5 1.7 copy-start.3
  176.4 44.8 %collective-permute-start.1 = (bf16[2,512,4,128]{3,1,2,0:T(8,128)(2,1)S(1)}, bf16[2,512,4,128]{3,1,2,0:T(8,128)(2,1)S(1)}, u32[]{:S(2)}, u32[]{:S(2)}) collective-permute-start(bf16[2,512,4,128]{3,1,2,0:T(8,128)(2,1)S(1)} %bitcast.116), channel_id=1, source_target_pairs={{2,0},{4,2},{6,4},{3,1},{5,3},{7,5},{10,8},{12,10},{14,12},{11,9},... | collective-permute-start | bytes 3145736 | tf_op jit(solution)/shard_map/ppermute | solution.py:14
  177.8 162.0 %all-gather.6.cloned.1.call-start = ((), (), s32[]{:S(2)}) async-start(), calls=%async_computation.2 | async-start | bytes 10485760 | tf_op jit(solution)/shard_map/all_gather | solution.py:99
  249.0 2.3 copy-start.6
  251.4 1.6 copy-start.11
  252.9 2.2 copy-start.8
  339.8 7.6 %copy-start.1 = (bf16[512,4,2,128]{3,2,1,0:T(2,128)(2,1)S(1)}, bf16[512,4,2,128]{3,2,1,0:T(2,128)(2,1)}, u32[]{:S(2)}) copy-start(bf16[512,4,2,128]{3,2,1,0:T(2,128)(2,1)} %param.6) | copy-start | bytes 3145732
Sparse Core Ops, SparseCore 0:
  10.2 44.1 all-gather.3
  177.9 71.0 all-reduce.1
  253.0 86.7 all-gather.5
